TPU v7x, 32 devices: a whole 2x2x4 slice. The times are simulated.
32 devices in a mesh: dp: 8 (over z, core), tensor: 4 (over y, x).
Axes of the slice: x: 2, y: 2, z: 4, core: 2. Of those that a mesh axis runs over, the one named last changes fastest.
Arguments:
- tokens: bfloat16 [8192, 2048], P(('dp', 'tensor')), may hold values from -6 to 6
- lengths: int32 [8, 3], P('dp'), may hold values from 1 to 512, 768 in all within a row
- query_weight: bfloat16 [2048, 2048], P('dp', 'tensor'), may hold values from -0.125 to 0.125
- key_weight: bfloat16 [2048, 2048], P('dp', 'tensor'), may hold values from -0.125 to 0.125
- value_weight: bfloat16 [2048, 2048], P('dp', 'tensor'), may hold values from -0.125 to 0.125
- output_weight: bfloat16 [2048, 2048], P('tensor', 'dp'), may hold values from -1.5 to 1.5
- gate_weight: bfloat16 [2048, 8192], P('dp', 'tensor'), may hold values from -0.125 to 0.125
- up_weight: bfloat16 [2048, 8192], P('dp', 'tensor'), may hold values from -0.125 to 0.125
- down_weight: bfloat16 [8192, 2048], P('tensor', 'dp'), may hold values from -0.0625 to 0.0625
- cotangent: bfloat16 [8192, 2048], P(('dp', 'tensor')), may hold values from -6 to 6
Outputs:
- output: bfloat16 [8192, 2048], P(('dp', 'tensor'))
- input_grad: bfloat16 [8192, 2048], P(('dp', 'tensor'))
- query_grad: float32 [2048, 2048], P('dp', 'tensor')
- key_grad: float32 [2048, 2048], P('dp', 'tensor')
- value_grad: float32 [2048, 2048], P('dp', 'tensor')
- output_grad: float32 [2048, 2048], P('tensor', 'dp')
- gate_grad: float32 [2048, 8192], P('dp', 'tensor')
- up_grad: float32 [2048, 8192], P('dp', 'tensor')
- down_grad: float32 [8192, 2048], P('tensor', 'dp')
Inputs may be any that keep to these rules, and one draw needn't show every extreme that they name: Each row holds the lengths of the 3 documents packed from the start of a slot of 1024 positions; the rest of the slot is padding. Every row's largest length is 512 and its lengths add to 768.
All inputs are finite; a program needn't handle non-finite values.
Results may differ from a plain program's by a relative error of at most 0.023.
Values may be sent and summed in bfloat16 or wider, within the bound.
No kernel may reach another device: no remote copies, remote signals or barrier semaphores. Data moves between devices by JAX's collectives and lax.ppermute only.
A program may use at most 256 MiB of HBM per device.

v0:
```python
import math
import jax
import jax.numpy as jnp
from jax import lax
from jax.sharding import PartitionSpec as P

HD = 128
QBLOCK = 512
EPSILON = 1e-05
ROPE_BASE = 10000.0
MASKED = -1e30


def layer_norm(rows):
    centre = jnp.mean(rows, axis=-1, keepdims=True)
    centered = rows - centre
    spread = jnp.mean(centered * centered, axis=-1, keepdims=True)
    return centered * lax.rsqrt(spread + EPSILON)


def slot_layout(lengths_row, row_total):
    ends = jnp.cumsum(lengths_row)
    places = jnp.arange(row_total, dtype=jnp.int32)
    segment = jnp.sum((places[:, None] >= ends[None, :]).astype(jnp.int32), axis=1)
    starts = jnp.concatenate([jnp.zeros((1,), jnp.int32), ends])
    picks = jnp.arange(starts.shape[0], dtype=jnp.int32)
    begins = jnp.sum(jnp.where(segment[:, None] == picks[None, :], starts[None, :], 0), axis=1)
    position = places - begins
    valid = (places < ends[-1]).astype(jnp.int32)
    return (segment, position, places, valid)


def rope_tables(position, head_size):
    half_size = head_size // 2
    steps_float = jnp.arange(half_size, dtype=jnp.float32)
    freqs = jnp.exp(steps_float * (-2.0 * math.log(ROPE_BASE) / head_size))
    angles = position.astype(jnp.float32)[:, None] * freqs[None, :]
    return (jnp.cos(angles), jnp.sin(angles))


def rotate(values, cosine_table, sine_table):
    half_size = values.shape[-1] // 2
    first_half = values[..., :half_size]
    second_half = values[..., half_size:]
    cosine_wide = cosine_table[:, None, :]
    sine_wide = sine_table[:, None, :]
    return jnp.concatenate(
        [
            first_half * cosine_wide - second_half * sine_wide,
            second_half * cosine_wide + first_half * sine_wide,
        ],
        axis=-1,
    )


def swish_product(gate_pre, up_pre):
    return jax.nn.silu(gate_pre) * up_pre


def dot_first(left, right):
    return lax.dot_general(
        left, right, (((0,), (0,)), ((), ())), preferred_element_type=jnp.float32
    )


def dot_last(left, right):
    return lax.dot_general(
        left, right, (((1,), (1,)), ((), ())), preferred_element_type=jnp.float32
    )


def block_scores(queries, keys_turned, segment_rows, segment_cols, place_rows, place_cols, scale):
    raw_scores = (
        jnp.einsum("qhd,khd->hqk", queries, keys_turned, preferred_element_type=jnp.float32) * scale
    )
    allowed = (segment_rows[:, None] == segment_cols[None, :]) & (
        place_rows[:, None] >= place_cols[None, :]
    )
    return jnp.where(allowed[None], raw_scores, MASKED)


def attend_forward(queries, keys_turned, values, segment, places, block_rows):
    slot_rows = queries.shape[0]
    scale = queries.shape[2] ** (-0.5)
    context_blocks = []
    log_totals = []
    for block_index in range(slot_rows // block_rows):
        lower_row = block_index * block_rows
        reach_row = lower_row + block_rows
        scores = block_scores(
            queries[lower_row:reach_row],
            keys_turned[:reach_row],
            segment[lower_row:reach_row],
            segment[:reach_row],
            places[lower_row:reach_row],
            places[:reach_row],
            scale,
        )
        row_peak = jnp.max(scores, axis=-1, keepdims=True)
        weights = jnp.exp(scores - row_peak)
        row_total = jnp.sum(weights, axis=-1, keepdims=True)
        probs = (weights / row_total).astype(jnp.bfloat16)
        context_blocks.append(
            jnp.einsum(
                "hqk,khd->qhd", probs, values[:reach_row], preferred_element_type=jnp.float32
            ).astype(jnp.bfloat16)
        )
        log_totals.append(row_peak + jnp.log(row_total))
    return (jnp.concatenate(context_blocks, axis=0), log_totals)


def attend_backward(
    queries, keys_turned, values, segment, places, log_totals, d_context, block_rows
):
    slot_rows, heads_here, head_size = queries.shape
    scale = head_size ** (-0.5)
    d_keys = jnp.zeros((slot_rows, heads_here, head_size), jnp.float32)
    d_values = jnp.zeros((slot_rows, heads_here, head_size), jnp.float32)
    d_query_blocks = []
    for block_index in range(slot_rows // block_rows):
        lower_row = block_index * block_rows
        reach_row = lower_row + block_rows
        query_block = queries[lower_row:reach_row]
        scores = block_scores(
            query_block,
            keys_turned[:reach_row],
            segment[lower_row:reach_row],
            segment[:reach_row],
            places[lower_row:reach_row],
            places[:reach_row],
            scale,
        )
        probs = jnp.exp(scores - log_totals[block_index])
        grads_block = d_context[lower_row:reach_row]
        d_probs = jnp.einsum(
            "qhd,khd->hqk", grads_block, values[:reach_row], preferred_element_type=jnp.float32
        )
        inner = jnp.sum(probs * d_probs, axis=-1, keepdims=True)
        d_scores = (probs * (d_probs - inner) * scale).astype(jnp.bfloat16)
        d_query_blocks.append(
            jnp.einsum(
                "hqk,khd->qhd",
                d_scores,
                keys_turned[:reach_row],
                preferred_element_type=jnp.float32,
            )
        )
        d_keys = d_keys.at[:reach_row].add(
            jnp.einsum("hqk,qhd->khd", d_scores, query_block, preferred_element_type=jnp.float32)
        )
        d_values = d_values.at[:reach_row].add(
            jnp.einsum(
                "hqk,qhd->khd",
                probs.astype(jnp.bfloat16),
                grads_block,
                preferred_element_type=jnp.float32,
            )
        )
    return (jnp.concatenate(d_query_blocks, axis=0), d_keys, d_values)


def per_device(
    tokens,
    lengths,
    query_weight,
    key_weight,
    value_weight,
    output_weight,
    gate_weight,
    up_weight,
    down_weight,
    cotangent,
):
    row_count = tokens.shape[0]
    slot_rows = row_count * lax.axis_size("tensor")
    first_row = lax.axis_index("tensor") * row_count
    segment, position, places, valid_all = slot_layout(lengths[0], slot_rows)
    valid_rows = lax.dynamic_slice_in_dim(valid_all, first_row, row_count, 0).astype(jnp.float32)[
        :, None
    ]
    cosine_table, sine_table = rope_tables(position, HD)
    heads_here = query_weight.shape[1] // HD
    weights = (
        lax.all_gather(query_weight, "dp", axis=0, tiled=True),
        lax.all_gather(key_weight, "dp", axis=0, tiled=True),
        lax.all_gather(value_weight, "dp", axis=0, tiled=True),
        lax.all_gather(output_weight, "dp", axis=1, tiled=True),
        lax.all_gather(gate_weight, "dp", axis=0, tiled=True),
        lax.all_gather(up_weight, "dp", axis=0, tiled=True),
        lax.all_gather(down_weight, "dp", axis=1, tiled=True),
    )
    residual_in = tokens.astype(jnp.float32)
    normed_one = layer_norm(residual_in).astype(jnp.bfloat16)
    gathered_one = lax.all_gather(normed_one, "tensor", axis=0, tiled=True)
    query_pre = jnp.dot(gathered_one, weights[0], preferred_element_type=jnp.float32).reshape(
        slot_rows, heads_here, HD
    )
    key_pre = jnp.dot(gathered_one, weights[1], preferred_element_type=jnp.float32).reshape(
        slot_rows, heads_here, HD
    )
    values = (
        jnp.dot(gathered_one, weights[2], preferred_element_type=jnp.float32)
        .astype(jnp.bfloat16)
        .reshape(slot_rows, heads_here, HD)
    )
    queries = rotate(query_pre, cosine_table, sine_table).astype(jnp.bfloat16)
    keys_turned = rotate(key_pre, cosine_table, sine_table).astype(jnp.bfloat16)
    context, log_totals = attend_forward(queries, keys_turned, values, segment, places, QBLOCK)
    context_flat = context.reshape(slot_rows, heads_here * HD)
    picked = context_flat
    attention_out = lax.psum_scatter(
        jnp.dot(picked, weights[3], preferred_element_type=jnp.float32).astype(jnp.bfloat16),
        "tensor",
        scatter_dimension=0,
        tiled=True,
    ).astype(jnp.float32)
    middle = residual_in + attention_out
    normed_two = layer_norm(middle).astype(jnp.bfloat16)
    gathered_two = lax.all_gather(normed_two, "tensor", axis=0, tiled=True)
    gate_pre = jnp.dot(gathered_two, weights[4], preferred_element_type=jnp.float32)
    up_pre = jnp.dot(gathered_two, weights[5], preferred_element_type=jnp.float32)
    hidden = swish_product(gate_pre, up_pre).astype(jnp.bfloat16)
    picked = hidden
    feed_out = lax.psum_scatter(
        jnp.dot(picked, weights[6], preferred_element_type=jnp.float32).astype(jnp.bfloat16),
        "tensor",
        scatter_dimension=0,
        tiled=True,
    ).astype(jnp.float32)
    output = (valid_rows * (middle + feed_out)).astype(jnp.bfloat16)
    weights = (
        lax.all_gather(query_weight, "dp", axis=0, tiled=True),
        lax.all_gather(key_weight, "dp", axis=0, tiled=True),
        lax.all_gather(value_weight, "dp", axis=0, tiled=True),
        lax.all_gather(output_weight, "dp", axis=1, tiled=True),
        lax.all_gather(gate_weight, "dp", axis=0, tiled=True),
        lax.all_gather(up_weight, "dp", axis=0, tiled=True),
        lax.all_gather(down_weight, "dp", axis=1, tiled=True),
    )
    masked_grad = valid_rows * cotangent.astype(jnp.float32)
    feed_grad = masked_grad.astype(jnp.bfloat16)
    rows_piece = lax.all_gather(feed_grad, "tensor", axis=0, tiled=True)
    picked = hidden
    down_part = dot_first(picked, rows_piece)
    hidden_part = dot_last(rows_piece, weights[6])
    _, swish_pull = jax.vjp(swish_product, gate_pre, up_pre)
    d_gate, d_up = swish_pull(hidden_part)
    d_gate = d_gate.astype(jnp.bfloat16)
    d_up = d_up.astype(jnp.bfloat16)
    gate_local = dot_first(gathered_two, d_gate)
    up_local = dot_first(gathered_two, d_up)
    d_normed_two = lax.psum_scatter(
        (dot_last(d_gate, weights[4]) + dot_last(d_up, weights[5])).astype(jnp.bfloat16),
        "tensor",
        scatter_dimension=0,
        tiled=True,
    ).astype(jnp.float32)
    _, second_pull = jax.vjp(layer_norm, middle)
    d_middle = masked_grad + second_pull(d_normed_two)[0]
    attention_grad = d_middle.astype(jnp.bfloat16)
    rows_piece = lax.all_gather(attention_grad, "tensor", axis=0, tiled=True)
    picked = context_flat
    weight_part = dot_first(picked, rows_piece)
    context_part = dot_last(rows_piece, weights[3])
    d_context = context_part
    d_context = d_context.astype(jnp.bfloat16).reshape(slot_rows, heads_here, HD)
    d_queries, d_keys, d_values = attend_backward(
        queries, keys_turned, values, segment, places, log_totals, d_context, QBLOCK
    )
    _, turn_pull = jax.vjp(lambda moved: rotate(moved, cosine_table, sine_table), query_pre)
    d_query_pre = turn_pull(d_queries)[0].astype(jnp.bfloat16).reshape(slot_rows, heads_here * HD)
    d_key_pre = turn_pull(d_keys)[0].astype(jnp.bfloat16).reshape(slot_rows, heads_here * HD)
    d_value_pre = d_values.astype(jnp.bfloat16).reshape(slot_rows, heads_here * HD)
    query_local = dot_first(gathered_one, d_query_pre)
    key_local = dot_first(gathered_one, d_key_pre)
    value_local = dot_first(gathered_one, d_value_pre)
    d_normed_one = lax.psum_scatter(
        (
            dot_last(d_query_pre, weights[0])
            + dot_last(d_key_pre, weights[1])
            + dot_last(d_value_pre, weights[2])
        ).astype(jnp.bfloat16),
        "tensor",
        scatter_dimension=0,
        tiled=True,
    ).astype(jnp.float32)
    _, first_pull = jax.vjp(layer_norm, residual_in)
    input_grad = (d_middle + first_pull(d_normed_one)[0]).astype(jnp.bfloat16)
    query_sum, key_sum, value_sum, output_sum, gate_sum, up_sum, down_sum = (
        lax.psum_scatter(
            query_local.astype(jnp.bfloat16), "dp", scatter_dimension=0, tiled=True
        ).astype(jnp.float32),
        lax.psum_scatter(
            key_local.astype(jnp.bfloat16), "dp", scatter_dimension=0, tiled=True
        ).astype(jnp.float32),
        lax.psum_scatter(
            value_local.astype(jnp.bfloat16), "dp", scatter_dimension=0, tiled=True
        ).astype(jnp.float32),
        lax.psum_scatter(
            weight_part.astype(jnp.bfloat16), "dp", scatter_dimension=1, tiled=True
        ).astype(jnp.float32),
        lax.psum_scatter(
            gate_local.astype(jnp.bfloat16), "dp", scatter_dimension=0, tiled=True
        ).astype(jnp.float32),
        lax.psum_scatter(
            up_local.astype(jnp.bfloat16), "dp", scatter_dimension=0, tiled=True
        ).astype(jnp.float32),
        lax.psum_scatter(
            down_part.astype(jnp.bfloat16), "dp", scatter_dimension=1, tiled=True
        ).astype(jnp.float32),
    )
    return (
        output,
        input_grad,
        query_sum,
        key_sum,
        value_sum,
        output_sum,
        gate_sum,
        up_sum,
        down_sum,
    )


def solution(mesh):
    return jax.shard_map(
        per_device,
        mesh=mesh,
        in_specs=(
            P(("dp", "tensor"), None),
            P("dp", None),
            P("dp", "tensor"),
            P("dp", "tensor"),
            P("dp", "tensor"),
            P("tensor", "dp"),
            P("dp", "tensor"),
            P("dp", "tensor"),
            P("tensor", "dp"),
            P(("dp", "tensor"), None),
        ),
        out_specs=(
            P(("dp", "tensor"), None),
            P(("dp", "tensor"), None),
            P("dp", "tensor"),
            P("dp", "tensor"),
            P("dp", "tensor"),
            P("tensor", "dp"),
            P("dp", "tensor"),
            P("dp", "tensor"),
            P("tensor", "dp"),
        ),
        check_vma=False,
    )
```

profile of v0, /device:TPU:0, one launch (start us, length us, event | category | flops | bytes accessed | tf_op | source)
XLA Modules:
  0.0 1302.9 jit_solution(14232833161550070507)
XLA Ops:
  22.0 19.5 %all-gather.18.cloned.1.call-done = bf16[2048,512]{1,0:T(8,128)(2,1)} async-done(((bf16[256,512]{1,0:T(8,128)(2,1)}), bf16[2048,512]{1,0:T(8,128)(2,1)}) %all-gather.18.cloned.1.call-update) | async-done | bytes 2097168 | tf_op jit(solution)/shard_map/all_gather | solution.py:185
  41.5 54.4 %all-gather.12.cloned.1.call-done = bf16[1024,2048]{1,0:T(8,128)(2,1)} async-done(((bf16[256,2048]{1,0:T(8,128)(2,1)}), bf16[1024,2048]{1,0:T(8,128)(2,1)}) %all-gather.12.cloned.1.call-update) | async-done | bytes 4194320 | tf_op jit(solution)/shard_map/all_gather | solution.py:194
  105.2 21.5 %all-gather.16.cloned.1.call-done = bf16[2048,512]{1,0:T(8,128)(2,1)} async-done(((bf16[256,512]{1,0:T(8,128)(2,1)}), bf16[2048,512]{1,0:T(8,128)(2,1)}) %all-gather.16.cloned.1.call-update) | async-done | bytes 2097168 | tf_op jit(solution)/shard_map/all_gather | solution.py:184
  195.0 51.0 %reduce-scatter.12.cloned.1.call-done = bf16[256,2048]{1,0:T(8,128)(2,1)} async-done(((bf16[1024,2048]{1,0:T(8,128)(2,1)}), bf16[256,2048]{1,0:T(8,128)(2,1)}) %reduce-scatter.12.cloned.1.call-update) | async-done | bytes 1048592 | tf_op jit(solution)/shard_map/reduce_scatter | solution.py:211
  255.1 74.6 %all-gather.26.cloned.1.call-done = bf16[2048,2048]{1,0:T(8,128)(2,1)} async-done(((bf16[256,2048]{1,0:T(8,128)(2,1)}), bf16[2048,2048]{1,0:T(8,128)(2,1)}) %all-gather.26.cloned.1.call-update) | async-done | bytes 8388624 | tf_op jit(solution)/shard_map/all_gather | solution.py:189
  329.7 53.5 %all-gather.22.cloned.1.call-done = bf16[1024,2048]{1,0:T(8,128)(2,1)} async-done(((bf16[256,2048]{1,0:T(8,128)(2,1)}), bf16[1024,2048]{1,0:T(8,128)(2,1)}) %all-gather.22.cloned.1.call-update) | async-done | bytes 4194320 | tf_op jit(solution)/shard_map/all_gather | solution.py:219
  383.2 14.8 %fusion.133 = f32[1024,2048]{1,0:T(8,128)} fusion(bf16[1024,2048]{1,0:T(8,128)(2,1)} %all-gather.22.cloned.1.call-done, bf16[2048,2048]{1,0:T(8,128)(2,1)} %all-gather.26.cloned.1.call-done), kind=kOutput, calls=%fused_computation.177 | convolution fusion | flops 8589934592 | bytes 20971520 | tf_op jit(solution)/shard_map/dot_general | solution.py:221
  398.0 68.9 %all-gather.24.cloned.1.call-done = bf16[2048,2048]{1,0:T(8,128)(2,1)} async-done(((bf16[256,2048]{1,0:T(8,128)(2,1)}), bf16[2048,2048]{1,0:T(8,128)(2,1)}) %all-gather.24.cloned.1.call-update) | async-done | bytes 8388624 | tf_op jit(solution)/shard_map/all_gather | solution.py:188
  466.9 14.4 %fusion.132 = f32[1024,2048]{1,0:T(8,128)} fusion(bf16[1024,2048]{1,0:T(8,128)(2,1)} %all-gather.22.cloned.1.call-done, bf16[2048,2048]{1,0:T(8,128)(2,1)} %all-gather.24.cloned.1.call-done), kind=kOutput, calls=%fused_computation.176 | convolution fusion | flops 8589934592 | bytes 20971520 | tf_op jit(solution)/shard_map/dot_general | solution.py:220
  481.3 39.0 %all-gather.30.cloned.1.call-done = bf16[1024,2048]{1,0:T(8,128)(2,1)} async-done(((bf16[256,2048]{1,0:T(8,128)(2,1)}), bf16[1024,2048]{1,0:T(8,128)(2,1)}) %all-gather.30.cloned.1.call-update) | async-done | bytes 4194320 | tf_op jit(solution)/shard_map/all_gather | solution.py:242
  520.3 84.1 %all-gather.28.cloned.1.call-done = bf16[2048,2048]{1,0:T(8,128)(2,1)} async-done(((bf16[2048,256]{1,0:T(8,128)(2,1)}), bf16[2048,2048]{1,0:T(8,128)(2,1)}) %all-gather.28.cloned.1.call-update) | async-done | bytes 8388624 | tf_op jit(solution)/shard_map/all_gather | solution.py:190
  604.4 21.7 %multiply_convert_fusion.1 = (bf16[1024,2048]{1,0:T(8,128)(2,1)}, bf16[1024,2048]{1,0:T(8,128)(2,1)}, bf16[1024,2048]{1,0:T(8,128)(2,1)}) fusion(f32[1024,2048]{1,0:T(8,128)} %fusion.132, f32[1024,2048]{1,0:T(8,128)} %fusion.133, bf16[1024,2048]{1,0:T(8,128)(2,1)} %all-gather.30.cloned.1.call-done, bf16[2048,2048]{1,0:T(8,128)(2,1)} %all-gather.28.cloned.1.call-done), kind=kOutput, calls=%fused_computation.12 | convolution fusion | flops 8623489024 | bytes 41943040 | tf_op jit(solution)/shard_map/dot_general | solution.py:67
  652.0 50.9 %reduce-scatter.16.cloned.1.call-done = bf16[256,2048]{1,0:T(8,128)(2,1)} async-done(((bf16[1024,2048]{1,0:T(8,128)(2,1)}), bf16[256,2048]{1,0:T(8,128)(2,1)}) %reduce-scatter.16.cloned.1.call-update) | async-done | bytes 1048592 | tf_op jit(solution)/shard_map/reduce_scatter | solution.py:252
  709.4 14.4 %convolution_convert_fusion.1 = bf16[2048,2048]{1,0:T(8,128)(2,1)} fusion(bf16[1024,2048]{1,0:T(8,128)(2,1)} %all-gather.22.cloned.1.call-done, bf16[1024,2048]{1,0:T(8,128)(2,1)} %get-tuple-element.73), kind=kOutput, calls=%fused_computation.20 | convolution fusion | flops 8594128896 | bytes 16777216 | tf_op jit(solution)/shard_map/dot_general | solution.py:61
  803.5 20.9 %fusion.89 = f32[512,4,128]{2,0,1:T(8,128)} fusion(f32[4,512,1024]{2,1,0:T(8,128)} %fusion.136, f32[4,512,1024]{2,1,0:T(8,128)} %copy-done.6, f32[4,512]{1,0:T(4,128)S(1)} %log_add_fusion, pred[512,1024]{1,0:T(8,128)(4,1)S(1)} %copy-done.20, bf16[1024,4,64]{2,0,1:T(8,128)(2,1)S(1)} %copy-done.13, bf16[1024,4,64]{2,0,1:T(8,128)(2,1)S(1)} %copy-done.11), kind=kOutput, calls=%fused_computation.113 | convolution fusion | flops 562039808 | bytes 19406848 | tf_op jit(solution)/shard_map/hqk,khd->qhd/dot_general | solution.py:141
  833.8 26.0 %bitcast_add_fusion.1 = f32[1024,4,128]{2,0,1:T(8,128)} fusion(f32[512,4,128]{2,0,1:T(8,128)S(1)} %copy-done.63, bf16[512,4,128]{2,0,1:T(8,128)(2,1)S(1)} %copy-done.25, f32[4,512,1024]{2,1,0:T(8,128)} %fusion.136, f32[4,512,1024]{2,1,0:T(8,128)} %copy-done.6, f32[4,512]{1,0:T(4,128)S(1)} %log_add_fusion, pred[512,1024]{1,0:T(8,128)(4,1)S(1)} %copy-done.20), kind=kOutput, calls=%fused_computation.79 | convolution fusion | flops 560466944 | bytes 20979712 | tf_op jit(solution)/shard_map/hqk,qhd->khd/dot_general | solution.py:149
  912.7 31.3 %reduce-scatter.28.cloned.1.call-done = bf16[256,2048]{1,0:T(8,128)(2,1)} async-done(((bf16[2048,2048]{1,0:T(8,128)(2,1)}), bf16[256,2048]{1,0:T(8,128)(2,1)}) %reduce-scatter.28.cloned.1.call-update) | async-done | bytes 1048592 | tf_op jit(solution)/shard_map/reduce_scatter | solution.py:302
  946.8 87.4 %reduce-scatter.32.cloned.1.call-done = bf16[2048,256]{1,0:T(8,128)(2,1)} async-done(((bf16[2048,2048]{1,0:T(8,128)(2,1)}), bf16[2048,256]{1,0:T(8,128)(2,1)}) %reduce-scatter.32.cloned.1.call-update) | async-done | bytes 1048592 | tf_op jit(solution)/shard_map/reduce_scatter | solution.py:308
  1036.9 34.0 %reduce-scatter.26.cloned.1.call-done = bf16[512,256]{1,0:T(8,128)(2,1)} async-done(((bf16[512,2048]{1,0:T(8,128)(2,1)}), bf16[512,256]{1,0:T(8,128)(2,1)}) %reduce-scatter.26.cloned.1.call-update) | async-done | bytes 262160 | tf_op jit(solution)/shard_map/reduce_scatter | solution.py:299
  1072.6 35.1 %reduce-scatter.24.cloned.1.call-done = bf16[256,512]{1,0:T(8,128)(2,1)} async-done(((bf16[2048,512]{1,0:T(8,128)(2,1)}), bf16[256,512]{1,0:T(8,128)(2,1)}) %reduce-scatter.24.cloned.1.call-update) | async-done | bytes 262160 | tf_op jit(solution)/shard_map/reduce_scatter | solution.py:296
  1109.5 35.2 %reduce-scatter.20.cloned.1.call-done = bf16[256,512]{1,0:T(8,128)(2,1)} async-done(((bf16[2048,512]{1,0:T(8,128)(2,1)}), bf16[256,512]{1,0:T(8,128)(2,1)}) %reduce-scatter.20.cloned.1.call-update) | async-done | bytes 262160 | tf_op jit(solution)/shard_map/reduce_scatter | solution.py:290
  1146.5 35.0 %reduce-scatter.22.cloned.1.call-done = bf16[256,512]{1,0:T(8,128)(2,1)} async-done(((bf16[2048,512]{1,0:T(8,128)(2,1)}), bf16[256,512]{1,0:T(8,128)(2,1)}) %reduce-scatter.22.cloned.1.call-update) | async-done | bytes 262160 | tf_op jit(solution)/shard_map/reduce_scatter | solution.py:293
  1183.3 52.4 %reduce-scatter.18.cloned.1.call-done = bf16[256,2048]{1,0:T(8,128)(2,1)} async-done(((bf16[1024,2048]{1,0:T(8,128)(2,1)}), bf16[256,2048]{1,0:T(8,128)(2,1)}) %reduce-scatter.18.cloned.1.call-update) | async-done | bytes 1048592 | tf_op jit(solution)/shard_map/reduce_scatter | solution.py:277
  1239.4 51.9 %reduce-scatter.14.cloned.1.call-done = bf16[256,2048]{1,0:T(8,128)(2,1)} async-done(((bf16[1024,2048]{1,0:T(8,128)(2,1)}), bf16[256,2048]{1,0:T(8,128)(2,1)}) %reduce-scatter.14.cloned.1.call-update) | async-done | bytes 1048592 | tf_op jit(solution)/shard_map/reduce_scatter | solution.py:224
  (275 shorter events, 295.5 us)
Async XLA Ops:
  7.2 34.3 %all-gather.18.cloned.1.call-start = ((), (), s32[]{:S(2)}) async-start(), calls=%async_computation.14 | async-start | bytes 2359296 | tf_op jit(solution)/shard_map/all_gather | solution.py:185
  7.9 88.0 %all-gather.12.cloned.1.call-start = ((), (), s32[]{:S(2)}) async-start(), calls=%async_computation.11 | async-start | bytes 5242880 | tf_op jit(solution)/shard_map/all_gather | solution.py:194
  14.7 112.0 %all-gather.16.cloned.1.call-start = ((), (), s32[]{:S(2)}) async-start(), calls=%async_computation.13 | async-start | bytes 2359296 | tf_op jit(solution)/shard_map/all_gather | solution.py:184
  15.5 141.3 %all-gather.14.cloned.1.call-start = ((), (), s32[]{:S(2)}) async-start(), calls=%async_computation.12 | async-start | bytes 2359296 | tf_op jit(solution)/shard_map/all_gather | solution.py:186
  16.1 172.2 %all-gather.20.cloned.1.call-start = ((), (), s32[]{:S(2)}) async-start(), calls=%async_computation.15 | async-start | bytes 2359296 | tf_op jit(solution)/shard_map/all_gather | solution.py:187
  16.6 229.4 %reduce-scatter.12.cloned.1.call-start = ((), (), s32[]{:S(2)}) async-start(), calls=%async_computation.16 | async-start | bytes 5242880 | tf_op jit(solution)/shard_map/reduce_scatter | solution.py:211
  194.2 135.5 %all-gather.26.cloned.1.call-start = ((), (), s32[]{:S(2)}) async-start(), calls=%async_computation.19 | async-start | bytes 9437184 | tf_op jit(solution)/shard_map/all_gather | solution.py:189
  195.0 188.2 %all-gather.22.cloned.1.call-start = ((), (), s32[]{:S(2)}) async-start(), calls=%async_computation.17 | async-start | bytes 5242880 | tf_op jit(solution)/shard_map/all_gather | solution.py:219
  247.7 459.1 %copy-start.39 = (f32[256]{0:T(256)}, f32[256]{0:T(256)S(1)}, u32[]{:S(2)}) copy-start(f32[256]{0:T(256)S(1)} %broadcast_multiply_fusion) | copy-start | bytes 3076
  249.5 457.3 %copy-start.47 = (f32[256]{0:T(256)}, f32[256]{0:T(256)S(1)}, u32[]{:S(2)}) copy-start(f32[256]{0:T(256)S(1)} %fusion.101) | copy-start | bytes 3076
  250.9 215.9 %all-gather.24.cloned.1.call-start = ((), (), s32[]{:S(2)}) async-start(), calls=%async_computation.18 | async-start | bytes 9437184 | tf_op jit(solution)/shard_map/all_gather | solution.py:188
  251.7 268.6 %all-gather.30.cloned.1.call-start = ((), (), s32[]{:S(2)}) async-start(), calls=%async_computation.22 | async-start | bytes 5242880 | tf_op jit(solution)/shard_map/all_gather | solution.py:242
  254.3 350.1 %all-gather.28.cloned.1.call-start = ((), (), s32[]{:S(2)}) async-start(), calls=%async_computation.20 | async-start | bytes 9437184 | tf_op jit(solution)/shard_map/all_gather | solution.py:190
  255.0 447.8 %reduce-scatter.16.cloned.1.call-start = ((), (), s32[]{:S(2)}) async-start(), calls=%async_computation.23 | async-start | bytes 5242880 | tf_op jit(solution)/shard_map/reduce_scatter | solution.py:252
  651.9 110.2 %all-gather.32.cloned.1.call-start = ((), (), s32[]{:S(2)}) async-start(), calls=%async_computation.24 | async-start | bytes 5242880 | tf_op jit(solution)/shard_map/all_gather | solution.py:261
  709.4 200.5 %reduce-scatter.30.cloned.1.call-start = ((), (), s32[]{:S(2)}) async-start(), calls=%async_computation.31 | async-start | bytes 9437184 | tf_op jit(solution)/shard_map/reduce_scatter | solution.py:305
  723.8 220.2 %reduce-scatter.28.cloned.1.call-start = ((), (), s32[]{:S(2)}) async-start(), calls=%async_computation.30 | async-start | bytes 9437184 | tf_op jit(solution)/shard_map/reduce_scatter | solution.py:302
  738.0 296.2 %reduce-scatter.32.cloned.1.call-start = ((), (), s32[]{:S(2)}) async-start(), calls=%async_computation.32 | async-start | bytes 9437184 | tf_op jit(solution)/shard_map/reduce_scatter | solution.py:308
  752.4 318.4 %reduce-scatter.26.cloned.1.call-start = ((), (), s32[]{:S(2)}) async-start(), calls=%async_computation.29 | async-start | bytes 2359296 | tf_op jit(solution)/shard_map/reduce_scatter | solution.py:299
  768.0 339.7 %reduce-scatter.24.cloned.1.call-start = ((), (), s32[]{:S(2)}) async-start(), calls=%async_computation.28 | async-start | bytes 2359296 | tf_op jit(solution)/shard_map/reduce_scatter | solution.py:296
  784.3 360.4 %reduce-scatter.20.cloned.1.call-start = ((), (), s32[]{:S(2)}) async-start(), calls=%async_computation.26 | async-start | bytes 2359296 | tf_op jit(solution)/shard_map/reduce_scatter | solution.py:290
  875.6 305.9 %reduce-scatter.22.cloned.1.call-start = ((), (), s32[]{:S(2)}) async-start(), calls=%async_computation.27 | async-start | bytes 2359296 | tf_op jit(solution)/shard_map/reduce_scatter | solution.py:293
  884.7 351.0 %reduce-scatter.18.cloned.1.call-start = ((), (), s32[]{:S(2)}) async-start(), calls=%async_computation.25 | async-start | bytes 5242880 | tf_op jit(solution)/shard_map/reduce_scatter | solution.py:277
  895.5 395.8 %reduce-scatter.14.cloned.1.call-start = ((), (), s32[]{:S(2)}) async-start(), calls=%async_computation.21 | async-start | bytes 5242880 | tf_op jit(solution)/shard_map/reduce_scatter | solution.py:224
  (65 other events, 3910.7 us)
Sparse Core Ops, SparseCore 0:
  9.6 31.8 all-gather.17
  43.9 51.9 all-gather.11
  97.5 29.1 all-gather.15
  128.2 28.5 all-gather.13
  158.2 30.0 all-gather.19
  194.4 51.6 reduce-scatter.11
  247.6 82.0 all-gather.25
  332.1 51.0 all-gather.21
  384.8 82.0 all-gather.23
  469.2 51.0 all-gather.29
  521.8 82.4 all-gather.27
  652.0 50.7 reduce-scatter.15
  709.5 52.5 all-gather.31
  764.3 89.5 reduce-scatter.29
  856.0 87.9 reduce-scatter.27
  946.1 87.9 reduce-scatter.31
  1036.3 34.5 reduce-scatter.25
  1073.0 34.6 reduce-scatter.23
  1110.0 34.6 reduce-scatter.19
  1146.8 34.5 reduce-scatter.21
  1184.4 51.2 reduce-scatter.17
  1238.7 52.5 reduce-scatter.13
where the time goes:
time: 1310 us; the launch traced here: 1300 us
  waiting for transfers between devices  921 us (70%)
  matrix products  281 us (21%)
  other arithmetic  67.1 us (5%)
  local copies, waits for them, and re-layouts  16.4 us (1%)
  between operations  15.6 us (1%)
    reduce_scatter x1, waiting for transfers between devices, per_device(): lax.psum_scatter(down_part.astype(jnp.bfloat16), 'dp', scatter_dimension=...  87.4 us
    all_gather x1, waiting for transfers between devices, per_device(): lax.all_gather(down_weight, 'dp', axis=1, tiled=True)  84.1 us
    all_gather x1, waiting for transfers between devices, per_device(): lax.all_gather(up_weight, 'dp', axis=0, tiled=True)  74.6 us
    all_gather x1, waiting for transfers between devices, per_device(): lax.all_gather(gate_weight, 'dp', axis=0, tiled=True)  68.9 us
    dot_general x7, matrix products, dot_first(): lax.dot_general(left, right, (((0,), (0,)), ((), ())), preferred_element_...  65 us
    dot_general x7, matrix products, dot_last(): lax.dot_general(left, right, (((1,), (1,)), ((), ())), preferred_element_...  64.1 us
    all_gather x1, waiting for transfers between devices, per_device(): gathered_one = lax.all_gather(normed_one, 'tensor', axis=0, tiled=True)  54.4 us
    all_gather x1, waiting for transfers between devices, per_device(): gathered_two = lax.all_gather(normed_two, 'tensor', axis=0, tiled=True)  53.5 us
  transfers between devices with their start and end apart: 22, of which 21 were waited for; matrix products, arithmetic and copies ran while one was open for 23% of the time, Pallas kernels for 0%

commit v1 on v0

--- a/solution.py
+++ b/solution.py
@@ -1,3 +1,4 @@
+import functools
 import math
 import jax
 import jax.numpy as jnp
@@ -9,6 +10,26 @@
 EPSILON = 1e-05
 ROPE_BASE = 10000.0
 MASKED = -1e30
+
+
+def obtain_the_zones(u, mesh_ax, pos_dim):
+    out_arr = jax.lax.axis_size(mesh_ax)
+    reached = jax.lax.axis_index(mesh_ax)
+    value_now, step_out = (out_arr, reached)
+    newest, formed = (u, 1)
+    while formed < value_now:
+        trail = []
+        for w in [*range(value_now)]:
+            trail.append((w, w ^ formed))
+        f_next = jax.lax.ppermute(newest, mesh_ax, trail)
+        prior = jnp.concatenate([newest, f_next], pos_dim)
+        item_now = jnp.concatenate([f_next, newest], axis=pos_dim)
+        newest = jnp.where(step_out & formed == 0, prior, item_now)
+        formed = 2 * formed
+    return newest
+
+
+region_push = functools.partial(obtain_the_zones, mesh_ax="dp", pos_dim=1)
 
 
 def layer_norm(rows):
@@ -187,7 +208,7 @@
         lax.all_gather(output_weight, "dp", axis=1, tiled=True),
         lax.all_gather(gate_weight, "dp", axis=0, tiled=True),
         lax.all_gather(up_weight, "dp", axis=0, tiled=True),
-        lax.all_gather(down_weight, "dp", axis=1, tiled=True),
+        region_push(down_weight),
     )
     residual_in = tokens.astype(jnp.float32)
     normed_one = layer_norm(residual_in).astype(jnp.bfloat16)

time: 1310 us -> 1520 us (1.16)
  waiting for transfers between devices: 921 us -> 1110 us
    ppermute x0 -> x3, waiting for transfers between devices: none -> 342 us  [obtain_the_zones(): f_next = jax.lax.ppermute(newest, mesh_ax, trail)]
    reduce_scatter x1, waiting for transfers between devices: 87.4 us -> 0.01 us  [per_device(): lax.psum_scatter(down_part.astype(jnp.bfloat16), 'dp', scatter_dimension=...]
    reduce_scatter x1, waiting for transfers between devices: 35.1 us -> 0.38 us  [per_device(): lax.psum_scatter(value_local.astype(jnp.bfloat16), 'dp', scatter_dimensio...]
    reduce_scatter x1, waiting for transfers between devices: 31.3 us -> 0.02 us  [per_device(): lax.psum_scatter(gate_local.astype(jnp.bfloat16), 'dp', scatter_dimension...]
  transfers between devices with their start and end apart: 22 -> 25, of which waited for: 21 -> 22; matrix products, arithmetic and copies ran while one was open for 23% -> 21% of each run, Pallas kernels for 0% -> 0%
where the time goes in v1:
time: 1520 us; the launch traced here: 1510 us
  waiting for transfers between devices  1110 us (73%)
  matrix products  291 us (19%)
  other arithmetic  75.2 us (5%)
  local copies, waits for them, and re-layouts  16.2 us (1%)
  between operations  15.7 us (1%)
    ppermute x3, waiting for transfers between devices, obtain_the_zones(): f_next = jax.lax.ppermute(newest, mesh_ax, trail)  342 us
    all_gather x1, waiting for transfers between devices, per_device(): lax.all_gather(down_weight, 'dp', axis=1, tiled=True)  84.1 us
    all_gather x1, waiting for transfers between devices, per_device(): lax.all_gather(gate_weight, 'dp', axis=0, tiled=True)  74.6 us
    all_gather x1, waiting for transfers between devices, per_device(): lax.all_gather(up_weight, 'dp', axis=0, tiled=True)  69.1 us
    dot_general x7, matrix products, dot_last(): lax.dot_general(left, right, (((1,), (1,)), ((), ())), preferred_element_...  65.8 us
    dot_general x7, matrix products, dot_first(): lax.dot_general(left, right, (((0,), (0,)), ((), ())), preferred_element_...  65.2 us
    all_gather x1, waiting for transfers between devices, per_device(): gathered_one = lax.all_gather(normed_one, 'tensor', axis=0, tiled=True)  54.4 us
    all_gather x1, waiting for transfers between devices, per_device(): gathered_two = lax.all_gather(normed_two, 'tensor', axis=0, tiled=True)  53.5 us
  transfers between devices with their start and end apart: 25, of which 22 were waited for; matrix products, arithmetic and copies ran while one was open for 21% of the time, Pallas kernels for 0%

profile of v1, /device:TPU:0, one launch (start us, length us, event | category | flops | bytes accessed | tf_op | source)
XLA Modules:
  0.0 1513.4 jit_solution(12460206742772263865)
XLA Ops:
  22.0 19.6 %all-gather.16.cloned.1.call-done = bf16[2048,512]{1,0:T(8,128)(2,1)} async-done(((bf16[256,512]{1,0:T(8,128)(2,1)}), bf16[2048,512]{1,0:T(8,128)(2,1)}) %all-gather.16.cloned.1.call-update) | async-done | bytes 2097168 | tf_op jit(solution)/shard_map/all_gather | solution.py:205
  41.5 54.4 %all-gather.12.cloned.1.call-done = bf16[1024,2048]{1,0:T(8,128)(2,1)} async-done(((bf16[256,2048]{1,0:T(8,128)(2,1)}), bf16[1024,2048]{1,0:T(8,128)(2,1)}) %all-gather.12.cloned.1.call-update) | async-done | bytes 4194320 | tf_op jit(solution)/shard_map/all_gather | solution.py:215
  103.3 23.5 %all-gather.18.cloned.1.call-done = bf16[2048,512]{1,0:T(8,128)(2,1)} async-done(((bf16[256,512]{1,0:T(8,128)(2,1)}), bf16[2048,512]{1,0:T(8,128)(2,1)}) %all-gather.18.cloned.1.call-update) | async-done | bytes 2097168 | tf_op jit(solution)/shard_map/all_gather | solution.py:206
  195.0 51.0 %reduce-scatter.12.cloned.1.call-done = bf16[256,2048]{1,0:T(8,128)(2,1)} async-done(((bf16[1024,2048]{1,0:T(8,128)(2,1)}), bf16[256,2048]{1,0:T(8,128)(2,1)}) %reduce-scatter.12.cloned.1.call-update) | async-done | bytes 1048592 | tf_op jit(solution)/shard_map/reduce_scatter | solution.py:232
  255.1 74.6 %all-gather.24.cloned.1.call-done = bf16[2048,2048]{1,0:T(8,128)(2,1)} async-done(((bf16[256,2048]{1,0:T(8,128)(2,1)}), bf16[2048,2048]{1,0:T(8,128)(2,1)}) %all-gather.24.cloned.1.call-update) | async-done | bytes 8388624 | tf_op jit(solution)/shard_map/all_gather | solution.py:209
  329.7 53.5 %all-gather.22.cloned.1.call-done = bf16[1024,2048]{1,0:T(8,128)(2,1)} async-done(((bf16[256,2048]{1,0:T(8,128)(2,1)}), bf16[1024,2048]{1,0:T(8,128)(2,1)}) %all-gather.22.cloned.1.call-update) | async-done | bytes 4194320 | tf_op jit(solution)/shard_map/all_gather | solution.py:240
  383.3 14.6 fusion.141
  397.9 69.1 %all-gather.26.cloned.1.call-done = bf16[2048,2048]{1,0:T(8,128)(2,1)} async-done(((bf16[256,2048]{1,0:T(8,128)(2,1)}), bf16[2048,2048]{1,0:T(8,128)(2,1)}) %all-gather.26.cloned.1.call-update) | async-done | bytes 8388624 | tf_op jit(solution)/shard_map/all_gather | solution.py:210
  466.9 14.5 fusion.142
  481.4 38.9 %all-gather.28.cloned.1.call-done = bf16[1024,2048]{1,0:T(8,128)(2,1)} async-done(((bf16[256,2048]{1,0:T(8,128)(2,1)}), bf16[1024,2048]{1,0:T(8,128)(2,1)}) %all-gather.28.cloned.1.call-update) | async-done | bytes 4194320 | tf_op jit(solution)/shard_map/all_gather | solution.py:263
  520.3 84.1 %all-gather.30.cloned.1.call-done = bf16[2048,2048]{1,0:T(8,128)(2,1)} async-done(((bf16[2048,256]{1,0:T(8,128)(2,1)}), bf16[2048,2048]{1,0:T(8,128)(2,1)}) %all-gather.30.cloned.1.call-update) | async-done | bytes 8388624 | tf_op jit(solution)/shard_map/all_gather | solution.py:259
  604.4 21.7 %multiply_convert_fusion.1 = (bf16[1024,2048]{1,0:T(8,128)(2,1)}, bf16[1024,2048]{1,0:T(8,128)(2,1)}, bf16[1024,2048]{1,0:T(8,128)(2,1)}) fusion(f32[1024,2048]{1,0:T(8,128)} %fusion.141, f32[1024,2048]{1,0:T(8,128)} %fusion.142, bf16[1024,2048]{1,0:T(8,128)(2,1)} %all-gather.28.cloned.1.call-done, bf16[2048,2048]{1,0:T(8,128)(2,1)} %all-gather.30.cloned.1.call-done), kind=kOutput, calls=%fused_computation.19 | convolution fusion | flops 8623489024 | bytes 41943040 | tf_op jit(solution)/shard_map/dot_general | solution.py:88
  626.1 14.9 fusion.143
  653.2 50.9 %reduce-scatter.16.cloned.1.call-done = bf16[256,2048]{1,0:T(8,128)(2,1)} async-done(((bf16[1024,2048]{1,0:T(8,128)(2,1)}), bf16[256,2048]{1,0:T(8,128)(2,1)}) %reduce-scatter.16.cloned.1.call-update) | async-done | bytes 1048592 | tf_op jit(solution)/shard_map/reduce_scatter | solution.py:273
  800.6 20.8 %fusion.97 = f32[512,4,128]{2,0,1:T(8,128)} fusion(f32[4,512,1024]{2,1,0:T(8,128)} %fusion.145, f32[4,512,1024]{2,1,0:T(8,128)} %copy-done.6, f32[4,512]{1,0:T(4,128)S(1)} %log_add_fusion, pred[512,1024]{1,0:T(8,128)(4,1)S(1)} %copy-done.20, bf16[1024,4,64]{2,0,1:T(8,128)(2,1)S(1)} %copy-done.13, bf16[1024,4,64]{2,0,1:T(8,128)(2,1)S(1)} %copy-done.11), kind=kOutput, calls=%fused_computation.123 | convolution fusion | flops 562039808 | bytes 19406848 | tf_op jit(solution)/shard_map/hqk,khd->qhd/dot_general | solution.py:162
  830.8 26.4 %bitcast_add_fusion.1 = f32[1024,4,128]{2,0,1:T(8,128)} fusion(f32[512,4,128]{2,0,1:T(8,128)S(1)} %copy-done.66, bf16[512,4,128]{2,0,1:T(8,128)(2,1)S(1)} %copy-done.25, f32[4,512,1024]{2,1,0:T(8,128)} %fusion.145, f32[4,512,1024]{2,1,0:T(8,128)} %copy-done.6, f32[4,512]{1,0:T(4,128)S(1)} %log_add_fusion, pred[512,1024]{1,0:T(8,128)(4,1)S(1)} %copy-done.20), kind=kOutput, calls=%fused_computation.89 | convolution fusion | flops 560466944 | bytes 20979712 | tf_op jit(solution)/shard_map/hqk,qhd->khd/dot_general | solution.py:170
  908.3 79.2 %collective-permute-done.1 = bf16[2048,512]{1,0:T(8,128)(2,1)} collective-permute-done((bf16[2048,512]{1,0:T(8,128)(2,1)S(1)}, bf16[2048,512]{1,0:T(8,128)(2,1)}, u32[]{:S(2)}, u32[]{:S(2)}) %collective-permute-start.1) | collective-permute-done | bytes 2097184 | tf_op jit(solution)/shard_map/ppermute | solution.py:24
  994.6 259.6 %collective-permute-done.2 = bf16[2048,1024]{1,0:T(8,128)(2,1)} collective-permute-done((bf16[2048,1024]{1,0:T(8,128)(2,1)}, bf16[2048,1024]{1,0:T(8,128)(2,1)}, u32[]{:S(2)}, u32[]{:S(2)}) %collective-permute-start.2) | collective-permute-done | bytes 4194336 | tf_op jit(solution)/shard_map/ppermute | solution.py:24
  1254.2 18.1 %fusion.49 = bf16[1024,2048]{1,0:T(8,128)(2,1)} fusion(bf16[1024,2048]{1,0:T(8,128)(2,1)} %get-tuple-element.75, bf16[2048,1024]{1,0:T(8,128)(2,1)} %collective-permute-done.2, bf16[2048,1024]{1,0:T(8,128)(2,1)} %maximum_select_fusion.2, pred[]{:T(512)S(6)} %eq.79), kind=kOutput, calls=%fused_computation.57 | convolution fusion | flops 8629780480 | bytes 16777216 | tf_op jit(solution)/shard_map/dot_general | solution.py:246
  1283.2 35.2 %reduce-scatter.22.cloned.1.call-done = bf16[256,512]{1,0:T(8,128)(2,1)} async-done(((bf16[2048,512]{1,0:T(8,128)(2,1)}), bf16[256,512]{1,0:T(8,128)(2,1)}) %reduce-scatter.22.cloned.1.call-update) | async-done | bytes 262160 | tf_op jit(solution)/shard_map/reduce_scatter | solution.py:314
  1320.2 34.9 %reduce-scatter.26.cloned.1.call-done = bf16[512,256]{1,0:T(8,128)(2,1)} async-done(((bf16[512,2048]{1,0:T(8,128)(2,1)}), bf16[512,256]{1,0:T(8,128)(2,1)}) %reduce-scatter.26.cloned.1.call-update) | async-done | bytes 262160 | tf_op jit(solution)/shard_map/reduce_scatter | solution.py:320
  1356.9 35.0 %reduce-scatter.20.cloned.1.call-done = bf16[256,512]{1,0:T(8,128)(2,1)} async-done(((bf16[2048,512]{1,0:T(8,128)(2,1)}), bf16[256,512]{1,0:T(8,128)(2,1)}) %reduce-scatter.20.cloned.1.call-update) | async-done | bytes 262160 | tf_op jit(solution)/shard_map/reduce_scatter | solution.py:311
  1393.7 52.4 %reduce-scatter.18.cloned.1.call-done = bf16[256,2048]{1,0:T(8,128)(2,1)} async-done(((bf16[1024,2048]{1,0:T(8,128)(2,1)}), bf16[256,2048]{1,0:T(8,128)(2,1)}) %reduce-scatter.18.cloned.1.call-update) | async-done | bytes 1048592 | tf_op jit(solution)/shard_map/reduce_scatter | solution.py:298
  1449.8 51.9 %reduce-scatter.14.cloned.1.call-done = bf16[256,2048]{1,0:T(8,128)(2,1)} async-done(((bf16[1024,2048]{1,0:T(8,128)(2,1)}), bf16[256,2048]{1,0:T(8,128)(2,1)}) %reduce-scatter.14.cloned.1.call-update) | async-done | bytes 1048592 | tf_op jit(solution)/shard_map/reduce_scatter | solution.py:245
  (284 shorter events, 299.0 us)
Async XLA Ops:
  7.2 34.3 %all-gather.16.cloned.1.call-start = ((), (), s32[]{:S(2)}) async-start(), calls=%async_computation.13 | async-start | bytes 2359296 | tf_op jit(solution)/shard_map/all_gather | solution.py:205
  7.9 88.0 %all-gather.12.cloned.1.call-start = ((), (), s32[]{:S(2)}) async-start(), calls=%async_computation.11 | async-start | bytes 5242880 | tf_op jit(solution)/shard_map/all_gather | solution.py:215
  14.8 111.9 %all-gather.18.cloned.1.call-start = ((), (), s32[]{:S(2)}) async-start(), calls=%async_computation.14 | async-start | bytes 2359296 | tf_op jit(solution)/shard_map/all_gather | solution.py:206
  15.5 141.2 %all-gather.14.cloned.1.call-start = ((), (), s32[]{:S(2)}) async-start(), calls=%async_computation.12 | async-start | bytes 2359296 | tf_op jit(solution)/shard_map/all_gather | solution.py:207
  16.1 172.1 %all-gather.20.cloned.1.call-start = ((), (), s32[]{:S(2)}) async-start(), calls=%async_computation.15 | async-start | bytes 2359296 | tf_op jit(solution)/shard_map/all_gather | solution.py:208
  16.7 229.4 %reduce-scatter.12.cloned.1.call-start = ((), (), s32[]{:S(2)}) async-start(), calls=%async_computation.16 | async-start | bytes 5242880 | tf_op jit(solution)/shard_map/reduce_scatter | solution.py:232
  194.2 135.5 %all-gather.24.cloned.1.call-start = ((), (), s32[]{:S(2)}) async-start(), calls=%async_computation.18 | async-start | bytes 9437184 | tf_op jit(solution)/shard_map/all_gather | solution.py:209
  195.0 188.3 %all-gather.22.cloned.1.call-start = ((), (), s32[]{:S(2)}) async-start(), calls=%async_computation.17 | async-start | bytes 5242880 | tf_op jit(solution)/shard_map/all_gather | solution.py:240
  251.0 215.9 %all-gather.26.cloned.1.call-start = ((), (), s32[]{:S(2)}) async-start(), calls=%async_computation.19 | async-start | bytes 9437184 | tf_op jit(solution)/shard_map/all_gather | solution.py:210
  251.8 268.5 %all-gather.28.cloned.1.call-start = ((), (), s32[]{:S(2)}) async-start(), calls=%async_computation.21 | async-start | bytes 5242880 | tf_op jit(solution)/shard_map/all_gather | solution.py:263
  254.4 350.0 %all-gather.30.cloned.1.call-start = ((), (), s32[]{:S(2)}) async-start(), calls=%async_computation.22 | async-start | bytes 9437184 | tf_op jit(solution)/shard_map/all_gather | solution.py:259
  255.1 449.0 %reduce-scatter.16.cloned.1.call-start = ((), (), s32[]{:S(2)}) async-start(), calls=%async_computation.23 | async-start | bytes 5242880 | tf_op jit(solution)/shard_map/reduce_scatter | solution.py:273
  653.2 110.2 %all-gather.32.cloned.1.call-start = ((), (), s32[]{:S(2)}) async-start(), calls=%async_computation.24 | async-start | bytes 5242880 | tf_op jit(solution)/shard_map/all_gather | solution.py:282
  710.6 561.7 %reduce-scatter.28.cloned.1.call-start = ((), (), s32[]{:S(2)}) async-start(), calls=%async_computation.30 | async-start | bytes 9437184 | tf_op jit(solution)/shard_map/reduce_scatter | solution.py:323
  725.2 550.0 %reduce-scatter.30.cloned.1.call-start = ((), (), s32[]{:S(2)}) async-start(), calls=%async_computation.31 | async-start | bytes 9437184 | tf_op jit(solution)/shard_map/reduce_scatter | solution.py:326
  739.4 538.7 %reduce-scatter.32.cloned.1.call-start = ((), (), s32[]{:S(2)}) async-start(), calls=%async_computation.32 | async-start | bytes 9437184 | tf_op jit(solution)/shard_map/reduce_scatter | solution.py:329
  753.7 527.5 %reduce-scatter.24.cloned.1.call-start = ((), (), s32[]{:S(2)}) async-start(), calls=%async_computation.28 | async-start | bytes 2359296 | tf_op jit(solution)/shard_map/reduce_scatter | solution.py:317
  781.0 537.4 %reduce-scatter.22.cloned.1.call-start = ((), (), s32[]{:S(2)}) async-start(), calls=%async_computation.27 | async-start | bytes 2359296 | tf_op jit(solution)/shard_map/reduce_scatter | solution.py:314
  872.8 482.4 %reduce-scatter.26.cloned.1.call-start = ((), (), s32[]{:S(2)}) async-start(), calls=%async_computation.29 | async-start | bytes 2359296 | tf_op jit(solution)/shard_map/reduce_scatter | solution.py:320
  878.7 513.2 %reduce-scatter.20.cloned.1.call-start = ((), (), s32[]{:S(2)}) async-start(), calls=%async_computation.26 | async-start | bytes 2359296 | tf_op jit(solution)/shard_map/reduce_scatter | solution.py:311
  887.9 558.2 %reduce-scatter.18.cloned.1.call-start = ((), (), s32[]{:S(2)}) async-start(), calls=%async_computation.25 | async-start | bytes 5242880 | tf_op jit(solution)/shard_map/reduce_scatter | solution.py:298
  894.1 93.4 %collective-permute-start.1 = (bf16[2048,512]{1,0:T(8,128)(2,1)S(1)}, bf16[2048,512]{1,0:T(8,128)(2,1)}, u32[]{:S(2)}, u32[]{:S(2)}) collective-permute-start(bf16[2048,512]{1,0:T(8,128)(2,1)S(1)} %maximum_select_fusion.5), channel_id=1, source_target_pairs={{0,8},{4,12},{8,0},{12,4},{16,24},{20,28},{24,16},{28,20},{1,9},{5... | collective-permute-start | bytes 6291464 | tf_op jit(solution)/shard_map/ppermute | solution.py:24
  907.9 593.7 %reduce-scatter.14.cloned.1.call-start = ((), (), s32[]{:S(2)}) async-start(), calls=%async_computation.20 | async-start | bytes 5242880 | tf_op jit(solution)/shard_map/reduce_scatter | solution.py:245
  992.5 261.7 %collective-permute-start.2 = (bf16[2048,1024]{1,0:T(8,128)(2,1)}, bf16[2048,1024]{1,0:T(8,128)(2,1)}, u32[]{:S(2)}, u32[]{:S(2)}) collective-permute-start(bf16[2048,1024]{1,0:T(8,128)(2,1)} %maximum_select_fusion.2), channel_id=1, source_target_pairs={{0,16},{4,20},{8,24},{12,28},{16,0},{20,4},{24,8},{28,12},{1,17},{... | collective-permute-start | bytes 12582920 | tf_op jit(solution)/shard_map/ppermute | solution.py:24
  (69 other events, 4018.4 us)
Sparse Core Ops, SparseCore 0:
  9.6 31.8 all-gather.15
  43.9 51.9 all-gather.11
  97.5 29.1 all-gather.17
  128.2 28.5 all-gather.13
  158.2 30.0 all-gather.19
  194.4 51.6 reduce-scatter.11
  247.7 82.0 all-gather.23
  332.2 51.0 all-gather.21
  384.9 82.0 all-gather.25
  469.2 51.0 all-gather.27
  521.9 82.4 all-gather.29
  653.3 50.7 reduce-scatter.15
  710.8 52.5 all-gather.31
  765.5 89.5 reduce-scatter.27
  857.2 132.6 reduce-scatter.29
  992.1 211.1 reduce-scatter.31
  1205.4 75.7 reduce-scatter.23
  1283.3 35.0 reduce-scatter.21
  1320.7 34.3 reduce-scatter.25
  1357.3 34.5 reduce-scatter.19
  1394.9 51.1 reduce-scatter.17
  1449.1 52.5 reduce-scatter.13
